TPU v7x, 256 devices: a whole 4x4x8 slice. The times are simulated.
256 devices in a mesh: band: 8 (over x_lo, y), sector: 32 (over x_hi, z, core).
Axes of the slice: x: 4 (x_hi: 2, x_lo: 2; x = x_hi * 2 + x_lo), y: 4, z: 8, core: 2. Of those that a mesh axis runs over, the one named last changes fastest.
Arguments:
- grid_lat: bfloat16 [64, 2048, 512], P('band', 'sector'), may hold values from -6 to 6
- mesh_lat: bfloat16 [32768, 512], P(('band', 'sector')), may hold values from -6 to 6
- edge_feat: bfloat16 [393216, 512], P(('band', 'sector')), may hold values from -24 to 24
- edge_src: int32 [393216], P(('band', 'sector')), may hold values from 0 to 255, as said below
- edge_dst: int32 [393216], P(('band', 'sector')), may hold values from 0 to 511, as said below
- send_rows: int32 [32768], P(('band', 'sector')), may hold values from 0 to 127
- w_edge1: bfloat16 [1536, 512], replicated, may hold values from -0.15625 to 0.15625
- w_edge2: bfloat16 [512, 512], replicated, may hold values from -0.25 to 0.25
- edge_gain: float32 [512], replicated, may hold values from 0.25 to 1.75
- w_node1: bfloat16 [1024, 512], replicated, may hold values from -0.1875 to 0.1875
- w_node2: bfloat16 [512, 512], replicated, may hold values from -0.25 to 0.25
- node_gain: float32 [512], replicated, may hold values from 0.25 to 1.75
- cotangent: bfloat16 [64, 2048, 512], P('band', 'sector'), may hold values from -6 to 6
Outputs:
- grid_out: bfloat16 [64, 2048, 512], P('band', 'sector')
- grad_grid: bfloat16 [64, 2048, 512], P('band', 'sector')
- grad_mesh: bfloat16 [32768, 512], P(('band', 'sector'))
- grad_w_edge1: float32 [1536, 512], P('sector')
Inputs may be any that keep to these rules, and one draw needn't show every extreme that they name: `edge_src`: A device's mesh table is its 128 own rows followed by 32 rows each from the sector neighbour below, the sector neighbour above, the band neighbour below and the band neighbour above; devices of the first band never read the rows from below, those of the last band never the rows from above. `edge_dst`: each grid point of a device is the destination of exactly 3 of that device's edges; edges are in no particular order.
All inputs are finite; a program needn't handle non-finite values.
Results may differ from a plain program's by a relative error of at most 0.02.
Values may be sent and summed in bfloat16 or wider, within the bound.
No kernel may reach another device: no remote copies, remote signals or barrier semaphores. Data moves between devices by JAX's collectives and lax.ppermute only.
A program may use at most 64 MiB of HBM per device.

v0:
```python
import math
import jax
import jax.numpy as jnp
from jax import lax
from jax.sharding import PartitionSpec as P

EPSILON = 1e-05


def with_halo(shard, sides, width, wrap):
    for axis, dim in sides:
        devices, length = (lax.axis_size(axis), shard.shape[dim])
        up = [(i, (i + 1) % devices) for i in range(devices if wrap else devices - 1)]
        down = [(j, i) for i, j in up]
        last = lax.slice_in_dim(shard, length - width, length, axis=dim)
        initial = lax.slice_in_dim(shard, 0, width, axis=dim)
        before = lax.ppermute(last, axis, up)
        after = lax.ppermute(initial, axis, down)
        shard = jnp.concatenate([before, shard, after], axis=dim)
    return shard


def swish(values):
    return values * jax.nn.sigmoid(values)


def layer_norm(values, gain_vector):
    average = jnp.mean(values, axis=-1, keepdims=True)
    centred = values - average
    spread = jnp.mean(centred * centred, axis=-1, keepdims=True)
    return centred * lax.rsqrt(spread + EPSILON) * gain_vector


def decode_tail(pre_act, grid_wide, edge_dst, w_edge2, edge_gain, w_node1, w_node2, node_gain):
    hidden = swish(pre_act).astype(jnp.bfloat16)
    edge_raw = jnp.dot(hidden, w_edge2, preferred_element_type=jnp.float32)
    message = layer_norm(edge_raw, edge_gain).astype(jnp.bfloat16)
    points = grid_wide.shape[0]
    onehot = (edge_dst[None, :] == jnp.arange(points, dtype=jnp.int32)[:, None]).astype(
        jnp.bfloat16
    )
    aggregated = jnp.dot(onehot, message, preferred_element_type=jnp.float32).astype(jnp.bfloat16)
    node_input = jnp.concatenate([aggregated, grid_wide.astype(jnp.bfloat16)], axis=1)
    node_hidden = swish(jnp.dot(node_input, w_node1, preferred_element_type=jnp.float32)).astype(
        jnp.bfloat16
    )
    node_raw = jnp.dot(node_hidden, w_node2, preferred_element_type=jnp.float32)
    return (grid_wide + layer_norm(node_raw, node_gain)).astype(jnp.bfloat16)


def shards(
    grid_lat,
    mesh_lat,
    edge_feat,
    edge_src,
    edge_dst,
    send_rows,
    w_edge1,
    w_edge2,
    edge_gain,
    w_node1,
    w_node2,
    node_gain,
    cotangent,
):
    feature_width = w_edge2.shape[0]
    lat_rows = grid_lat.shape[0]
    lon_cols = grid_lat.shape[1]
    grid_block = grid_lat.reshape(lat_rows * lon_cols, feature_width)
    cot_block = cotangent.reshape(lat_rows * lon_cols, feature_width)
    own_rows = mesh_lat.shape[0]
    margin = send_rows.shape[0] // 4
    picked = jnp.take(mesh_lat, send_rows, axis=0)
    sector_recv = with_halo(picked[: 2 * margin], (("sector", 0),), margin, True)
    band_recv = with_halo(picked[2 * margin :], (("band", 0),), margin, False)
    mesh_table = jnp.concatenate(
        [
            mesh_lat,
            sector_recv[:margin],
            sector_recv[3 * margin :],
            band_recv[:margin],
            band_recv[3 * margin :],
        ],
        axis=0,
    )
    inputs = jnp.concatenate([edge_feat, mesh_table[edge_src], grid_block[edge_dst]], axis=1)
    pre_act = jnp.dot(inputs, w_edge1, preferred_element_type=jnp.float32)
    grid_wide = grid_block.astype(jnp.float32)

    def finish(pre_values, grid_values):
        return decode_tail(
            pre_values, grid_values, edge_dst, w_edge2, edge_gain, w_node1, w_node2, node_gain
        )

    result, pullback = jax.vjp(finish, pre_act, grid_wide)
    grad_pre, grad_tail = pullback(cot_block)
    grad_pre_b = grad_pre.astype(jnp.bfloat16)
    grad_inputs = lax.dot_general(
        grad_pre_b,
        w_edge1[feature_width:],
        (((1,), (1,)), ((), ())),
        preferred_element_type=jnp.float32,
    )
    grad_table = jax.ops.segment_sum(
        grad_inputs[:, :feature_width], edge_src, num_segments=mesh_table.shape[0]
    )
    grad_grid = grad_tail + jax.ops.segment_sum(
        grad_inputs[:, feature_width:], edge_dst, num_segments=grid_block.shape[0]
    )
    sector_back = with_halo(
        grad_table[own_rows : own_rows + 2 * margin].astype(jnp.bfloat16),
        (("sector", 0),),
        margin,
        True,
    ).astype(jnp.float32)
    band_back = with_halo(
        grad_table[own_rows + 2 * margin :].astype(jnp.bfloat16), (("band", 0),), margin, False
    ).astype(jnp.float32)
    returned = jnp.concatenate(
        [
            sector_back[:margin],
            sector_back[3 * margin :],
            band_back[:margin],
            band_back[3 * margin :],
        ],
        axis=0,
    )
    grad_mesh = (
        grad_table[:own_rows] + jax.ops.segment_sum(returned, send_rows, num_segments=own_rows)
    ).astype(jnp.bfloat16)
    total_edges = edge_feat.shape[0] * lax.axis_size("band") * lax.axis_size("sector")
    grad_scale = 1.0 / math.sqrt(total_edges)
    rows_out = 3 * feature_width // lax.axis_size("sector")
    full_grad = lax.dot_general(
        inputs, grad_pre_b, (((0,), (0,)), ((), ())), preferred_element_type=jnp.float32
    )
    summed = lax.psum(full_grad, ("band", "sector"))
    share_rows = lax.dynamic_slice_in_dim(summed, lax.axis_index("sector") * rows_out, rows_out, 0)
    grad_w_edge1 = share_rows * grad_scale
    grid_out = result.reshape(lat_rows, lon_cols, feature_width)
    grad_grid_out = grad_grid.astype(jnp.bfloat16).reshape(lat_rows, lon_cols, feature_width)
    return (grid_out, grad_grid_out, grad_mesh, grad_w_edge1)


def solution(mesh):
    in_specs = (
        P("band", "sector", None),
        P(("band", "sector"), None),
        P(("band", "sector"), None),
        P(("band", "sector")),
        P(("band", "sector")),
        P(("band", "sector")),
        P(),
        P(),
        P(),
        P(),
        P(),
        P(),
        P("band", "sector", None),
    )
    out_specs = (
        P("band", "sector", None),
        P("band", "sector", None),
        P(("band", "sector"), None),
        P("sector", None),
    )
    return jax.shard_map(shards, mesh=mesh, in_specs=in_specs, out_specs=out_specs, check_vma=False)
```

profile of v0, /device:TPU:2, one launch (start us, length us, event | category | flops | bytes accessed | tf_op | source)
XLA Modules:
  0.0 343.9 jit_solution(3824243465645055062)
XLA Ops:
  8.7 1.8 gather_fusion
  11.2 6.9 %collective-permute-start.1 = (bf16[32,512]{1,0:T(8,128)(2,1)}, bf16[32,512]{1,0:T(8,128)(2,1)S(1)}, u32[]{:S(2)}, u32[]{:S(2)}) collective-permute-start(bf16[32,512]{1,0:T(8,128)(2,1)} %get-tuple-element.21), channel_id=1, source_target_pairs={{1,0},{2,1},{3,2},{4,3},{5,4},{6,5},{7,6},{8,7},{9,8},{10,9},{11,1... | collective-permute-start | bytes 98312 | tf_op jit(solution)/shard_map/ppermute | solution.py:18
  18.1 3.5 %collective-permute-start.2 = (bf16[32,512]{1,0:T(8,128)(2,1)}, bf16[32,512]{1,0:T(8,128)(2,1)S(1)}, u32[]{:S(2)}, u32[]{:S(2)}) collective-permute-start(bf16[32,512]{1,0:T(8,128)(2,1)} %get-tuple-element.20), channel_id=1, source_target_pairs={{0,32},{32,64},{64,96},{96,128},{128,160},{160,192},{192,224},{1,3... | collective-permute-start | bytes 98312 | tf_op jit(solution)/shard_map/ppermute | solution.py:17
  21.6 4.5 %collective-permute-start.3 = (bf16[32,512]{1,0:T(8,128)(2,1)}, bf16[32,512]{1,0:T(8,128)(2,1)S(1)}, u32[]{:S(2)}, u32[]{:S(2)}) collective-permute-start(bf16[32,512]{1,0:T(8,128)(2,1)} %get-tuple-element.19), channel_id=1, source_target_pairs={{32,0},{64,32},{96,64},{128,96},{160,128},{192,160},{224,192},{33,... | collective-permute-start | bytes 98312 | tf_op jit(solution)/shard_map/ppermute | solution.py:18
  27.0 2.7 constant_dynamic-update-slice_fusion.7
  29.7 4.8 %gather_fusion.2 = bf16[1536,512]{1,0:T(8,128)(2,1)S(1)} fusion(bf16[512,512]{1,0:T(8,128)(2,1)S(1)} %bitcast.21, s32[2048]{0:T(1024)S(1)} %pad_clamp_fusion), kind=kCustom, calls=%fused_computation.2 | custom fusion | bytes 3151872 | tf_op jit(solution)/shard_map/gather | solution.py:86
  34.7 5.4 %gather_fusion.1 = bf16[1536,512]{1,0:T(8,128)(2,1)} fusion(bf16[256,512]{1,0:T(8,128)(2,1)S(1)} %constant_dynamic-update-slice_fusion, s32[2048]{0:T(1024)S(1)} %pad_clamp_fusion.1), kind=kCustom, calls=%fused_computation.1 | custom fusion | bytes 3151872 | tf_op jit(solution)/shard_map/gather | solution.py:86
  40.1 2.8 constant_dynamic-update-slice_fusion.6
  42.9 1.3 constant_dynamic-update-slice_fusion.5
  44.2 4.5 %fusion.69 = f32[1536,512]{1,0:T(8,128)S(1)} fusion(bf16[1536,1536]{1,0:T(8,128)(2,1)} %constant_dynamic-update-slice_fusion.5, bf16[1536,512]{1,0:T(8,128)(2,1)S(1)} %copy-done.10), kind=kOutput, calls=%fused_computation.121 | convolution fusion | flops 2415919104 | bytes 9437184 | tf_op jit(solution)/shard_map/dot_general | solution.py:87
  55.2 1.3 fusion.63
  56.5 3.6 %convolution_convert_fusion = bf16[512,1024]{1,0:T(8,128)(2,1)} fusion(bf16[1024,512]{1,0:T(8,128)(2,1)S(1)} %copy-done, f32[512,512]{1,0:T(8,128)} %copy-done.15, bf16[512,512]{1,0:T(8,128)(2,1)} %param.23, f32[512,512]{1,0:T(8,128)S(1)} %get-tuple-element.7, f32[512]{0:T(512)S(1)} %negate_multiply_fusion.1), kind=kOutput, calls=%fused_computation.39 | convolution fusion | flops 808976384 | bytes 4720640 | tf_op jit(solution)/shard_map/transpose(jvp())/dot_general | solution.py:44
  60.1 3.5 %multiply_reduce_fusion = (f32[1536]{0:T(1024)S(1)}, bf16[1536,512]{0,1:T(8,128)(2,1)S(1)}) fusion(f32[1536,512]{0,1:T(8,128)} %copy-done.2, f32[512]{0:T(512)S(1)} %copy-done.9, f32[1536]{0:T(1024)S(1)} %broadcast_multiply_fusion, bf16[512,1024]{1,0:T(8,128)(2,1)} %convolution_convert_fusion, s32[1536]{0:T(1024)S(1)} %copy-done.8), kind=kOutput, calls=%fused_computation.19 | convolution fusion | flops 810809856 | bytes 5263360 | tf_op jit(solution)/shard_map/transpose(jvp())/dot_general | solution.py:42
  65.7 2.6 fusion.1
  69.5 4.3 %fusion.70 = f32[1536,512]{1,0:T(8,128)} fusion(bf16[1536,1536]{1,0:T(8,128)(2,1)S(1)} %bitcast.26, bf16[1536,512]{1,0:T(8,128)(2,1)S(1)} %fusion.1), kind=kOutput, calls=%fused_computation.122 | convolution fusion | flops 2415919104 | bytes 9437184 | tf_op jit(solution)/shard_map/dot_general | solution.py:134
  73.8 6.2 %fusion.36 = f32[1536,1024]{1,0:T(8,128)} fusion(bf16[1536,512]{1,0:T(8,128)(2,1)} %copy-done.14, bf16[1536,512]{1,0:T(8,128)(2,1)} %param.19), kind=kOutput, calls=%fused_computation.55 | convolution fusion | flops 1610612736 | bytes 8912896 | tf_op jit(solution)/shard_map/dot_general | solution.py:98
  80.0 10.6 %scatter_custom_fusion.1 = f32[256,512]{1,0:T(8,128)S(1)} fusion(s32[1536]{0:T(1024)} %param.16, f32[1536,1024]{1,0:T(8,128)} %fusion.36, f32[]{:T(128)} %constant.22.clone.1), kind=kCustom, calls=%fused_computation.13 | custom fusion | flops 786432 | bytes 3670528 | tf_op jit(solution)/shard_map/scatter-add | solution.py:104
  90.6 3.7 %collective-permute-start.7 = (bf16[32,512]{1,0:T(8,128)(2,1)S(1)}, bf16[32,512]{1,0:T(8,128)(2,1)S(1)}, u32[]{:S(2)}, u32[]{:S(2)}) collective-permute-start(bf16[32,512]{1,0:T(8,128)(2,1)S(1)} %get-tuple-element.10), channel_id=1, source_target_pairs={{32,0},{64,32},{96,64},{128,96},{160,128},{192,160},{224,192},{33,... | collective-permute-start | bytes 98312 | tf_op jit(solution)/shard_map/ppermute | solution.py:18
  94.3 2.2 collective-permute-start.6
  97.7 10.9 %scatter_custom_fusion = f32[512,512]{1,0:T(8,128)S(1)} fusion(f32[512,512]{1,0:T(8,128)S(1)} %convert_add_fusion, s32[1536]{0:T(1024)S(1)} %copy-done.8, f32[1536,1024]{1,0:T(8,128)} %fusion.36), kind=kCustom, calls=%fused_computation.15 | custom fusion | flops 786432 | bytes 4194304 | tf_op jit(solution)/shard_map/scatter-add | solution.py:107
  111.1 5.4 %collective-permute-done.4 = bf16[32,512]{1,0:T(8,128)(2,1)S(1)} collective-permute-done((bf16[32,512]{1,0:T(8,128)(2,1)S(1)}, bf16[32,512]{1,0:T(8,128)(2,1)S(1)}, u32[]{:S(2)}, u32[]{:S(2)}) %collective-permute-start.4) | collective-permute-done | bytes 32800 | tf_op jit(solution)/shard_map/ppermute | solution.py:17
  116.5 1.6 scatter_custom_fusion.2
  118.8 216.7 %all-reduce.2.cloned.1.call-done = f32[1536,512]{1,0:T(8,128)} async-done(((f32[1536,512]{1,0:T(8,128)}), f32[1536,512]{1,0:T(8,128)}) %all-reduce.2.cloned.1.call-update) | async-done | bytes 3145744 | tf_op jit(solution)/shard_map/psum | solution.py:137
  335.5 1.5 dynamic-slice_multiply_fusion
  (90 shorter events, 17.2 us)
Async XLA Ops:
  7.2 45.1 %copy-start = (bf16[1024,512]{1,0:T(8,128)(2,1)S(1)}, bf16[1024,512]{1,0:T(8,128)(2,1)}, u32[]{:S(2)}) copy-start(bf16[1024,512]{1,0:T(8,128)(2,1)} %param.22) | copy-start | bytes 3145732
  7.2 22.5 %copy-start.6 = (s32[1536]{0:T(1024)S(1)}, s32[1536]{0:T(1024)}, u32[]{:S(2)}) copy-start(s32[1536]{0:T(1024)} %param.16) | copy-start | bytes 18436
  7.2 22.5 %copy-start.7 = (s32[1536]{0:T(1024)S(1)}, s32[1536]{0:T(1024)}, u32[]{:S(2)}) copy-start(s32[1536]{0:T(1024)} %param.17) | copy-start | bytes 18436
  7.2 22.5 %copy-start.1 = (bf16[8,64,512]{2,1,0:T(8,128)(2,1)S(1)}, bf16[8,64,512]{2,1,0:T(8,128)(2,1)}, u32[]{:S(2)}) copy-start(bf16[8,64,512]{2,1,0:T(8,128)(2,1)} %param.13) | copy-start | bytes 1572868
  7.2 328.3 %all-reduce.2.cloned.1.call-start = ((), (), s32[]{:S(2)}) async-start(), calls=%async_computation | async-start | bytes 6291456 | tf_op jit(solution)/shard_map/psum | solution.py:137
  11.2 23.3 %collective-permute-start = (bf16[32,512]{1,0:T(8,128)(2,1)}, bf16[32,512]{1,0:T(8,128)(2,1)S(1)}, u32[]{:S(2)}, u32[]{:S(2)}) collective-permute-start(bf16[32,512]{1,0:T(8,128)(2,1)} %get-tuple-element.22), channel_id=1, source_target_pairs={{0,1},{1,2},{2,3},{3,4},{4,5},{5,6},{6,7},{7,8},{8,9},{9,10},{10,1... | collective-permute-start | bytes 98312 | tf_op jit(solution)/shard_map/ppermute | solution.py:17
  11.2 23.3 %collective-permute-start.1 = (bf16[32,512]{1,0:T(8,128)(2,1)}, bf16[32,512]{1,0:T(8,128)(2,1)S(1)}, u32[]{:S(2)}, u32[]{:S(2)}) collective-permute-start(bf16[32,512]{1,0:T(8,128)(2,1)} %get-tuple-element.21), channel_id=1, source_target_pairs={{1,0},{2,1},{3,2},{4,3},{5,4},{6,5},{7,6},{8,7},{9,8},{10,9},{11,1... | collective-permute-start | bytes 98312 | tf_op jit(solution)/shard_map/ppermute | solution.py:18
  18.1 16.5 %collective-permute-start.2 = (bf16[32,512]{1,0:T(8,128)(2,1)}, bf16[32,512]{1,0:T(8,128)(2,1)S(1)}, u32[]{:S(2)}, u32[]{:S(2)}) collective-permute-start(bf16[32,512]{1,0:T(8,128)(2,1)} %get-tuple-element.20), channel_id=1, source_target_pairs={{0,32},{32,64},{64,96},{96,128},{128,160},{160,192},{192,224},{1,3... | collective-permute-start | bytes 98312 | tf_op jit(solution)/shard_map/ppermute | solution.py:17
  21.6 13.1 %collective-permute-start.3 = (bf16[32,512]{1,0:T(8,128)(2,1)}, bf16[32,512]{1,0:T(8,128)(2,1)S(1)}, u32[]{:S(2)}, u32[]{:S(2)}) collective-permute-start(bf16[32,512]{1,0:T(8,128)(2,1)} %get-tuple-element.19), channel_id=1, source_target_pairs={{32,0},{64,32},{96,64},{128,96},{160,128},{192,160},{224,192},{33,... | collective-permute-start | bytes 98312 | tf_op jit(solution)/shard_map/ppermute | solution.py:18
  40.1 4.1 %copy-start.10 = (bf16[1536,512]{1,0:T(8,128)(2,1)S(1)}, bf16[1536,512]{1,0:T(8,128)(2,1)}, u32[]{:S(2)}) copy-start(bf16[1536,512]{1,0:T(8,128)(2,1)} %param.19) | copy-start | bytes 4718596
  44.2 4.5 %copy-start.12 = (bf16[512,512]{1,0:T(8,128)(2,1)S(1)}, bf16[512,512]{1,0:T(8,128)(2,1)}, u32[]{:S(2)}) copy-start(bf16[512,512]{1,0:T(8,128)(2,1)} %param.20) | copy-start | bytes 1572868
  48.7 1.6 copy-start.16
  50.4 1.9 copy-start.2
  53.3 1.4 copy-start.4
  53.4 1.4 copy-start.5
  60.1 3.5 %copy-start.3 = (f32[1536,512]{0,1:T(8,128)S(1)}, f32[1536,512]{0,1:T(8,128)}, u32[]{:S(2)}) copy-start(f32[1536,512]{0,1:T(8,128)} %copy-done.2) | copy-start | bytes 9437188
  63.6 2.1 copy-start.17
  63.7 5.8 %slice-start = ((s8[4718592]{0:T(1024)(128)(4,1)}), s8[4194304]{0:T(1024)(128)(4,1)S(1)}, s32[]{:S(2)}) async-start(s8[4718592]{0:T(1024)(128)(4,1)} %bitcast.25), calls=%async_computation.1 | async-start | bytes 8388608
  65.7 3.8 %slice-start.1 = ((s8[4718592]{0:T(1024)(128)(4,1)}), s8[524288]{0:T(1024)(128)(4,1)S(1)}, s32[]{:S(2)}) async-start(s8[4718592]{0:T(1024)(128)(4,1)} %bitcast.25), calls=%async_computation.2 | async-start | bytes 1048576
  68.3 1.2 copy-start.14
  90.6 19.4 %collective-permute-start.7 = (bf16[32,512]{1,0:T(8,128)(2,1)S(1)}, bf16[32,512]{1,0:T(8,128)(2,1)S(1)}, u32[]{:S(2)}, u32[]{:S(2)}) collective-permute-start(bf16[32,512]{1,0:T(8,128)(2,1)S(1)} %get-tuple-element.10), channel_id=1, source_target_pairs={{32,0},{64,32},{96,64},{128,96},{160,128},{192,160},{224,192},{33,... | collective-permute-start | bytes 98312 | tf_op jit(solution)/shard_map/ppermute | solution.py:18
  94.3 15.7 %collective-permute-start.6 = (bf16[32,512]{1,0:T(8,128)(2,1)S(1)}, bf16[32,512]{1,0:T(8,128)(2,1)S(1)}, u32[]{:S(2)}, u32[]{:S(2)}) collective-permute-start(bf16[32,512]{1,0:T(8,128)(2,1)S(1)} %get-tuple-element.11), channel_id=1, source_target_pairs={{0,32},{32,64},{64,96},{96,128},{128,160},{160,192},{192,224},{1,3... | collective-permute-start | bytes 98312 | tf_op jit(solution)/shard_map/ppermute | solution.py:17
  109.5 1.6 collective-permute-start.5
  109.5 7.0 %collective-permute-start.4 = (bf16[32,512]{1,0:T(8,128)(2,1)S(1)}, bf16[32,512]{1,0:T(8,128)(2,1)S(1)}, u32[]{:S(2)}, u32[]{:S(2)}) collective-permute-start(bf16[32,512]{1,0:T(8,128)(2,1)S(1)} %get-tuple-element.9), channel_id=1, source_target_pairs={{0,1},{1,2},{2,3},{3,4},{4,5},{5,6},{6,7},{7,8},{8,9},{9,10},{10,1... | collective-permute-start | bytes 98312 | tf_op jit(solution)/shard_map/ppermute | solution.py:17
  (5 other events, 4.5 us)
Sparse Core Ops, SparseCore 0:
  73.9 261.5 all-reduce.1
where the time goes:
time: 344 us
  waiting for transfers between devices  223 us (65%)
  other arithmetic  32 us (9%)
  matrix products  28.2 us (8%)
  local copies, waits for them, and re-layouts  24.8 us (7%)
  starting transfers between devices  21.2 us (6%)
  between operations  14.5 us (4%)
    psum x1, waiting for transfers between devices, shards(): summed = lax.psum(full_grad, ('band', 'sector'))  217 us
    ppermute x4, starting transfers between devices, with_halo(): after = lax.ppermute(initial, axis, down)  15 us
    scatter-add x1, other arithmetic, shards(): jax.ops.segment_sum(grad_inputs[:, feature_width:], edge_dst, num_segment...  10.9 us
    unnamed x46, local copies, waits for them, and re-layouts  10.8 us
    scatter-add x1, other arithmetic, shards(): jax.ops.segment_sum(grad_inputs[:, :feature_width], edge_src, num_segment...  10.6 us
  transfers between devices with their start and end apart: 9, of which 3 were waited for; matrix products, arithmetic and copies ran while one was open for 12% of the time, Pallas kernels for 0%

commit v1 on v0

--- a/solution.py
+++ b/solution.py
@@ -134,7 +134,9 @@
     full_grad = lax.dot_general(
         inputs, grad_pre_b, (((0,), (0,)), ((), ())), preferred_element_type=jnp.float32
     )
-    summed = lax.psum(full_grad, ("band", "sector"))
+    summed = full_grad
+    for over in ("sector", "band"):
+        summed = lax.psum(summed, over)
     share_rows = lax.dynamic_slice_in_dim(summed, lax.axis_index("sector") * rows_out, rows_out, 0)
     grad_w_edge1 = share_rows * grad_scale
     grid_out = result.reshape(lat_rows, lon_cols, feature_width)

time: 344 us -> 452 us (1.31)
  waiting for transfers between devices: 223 us -> 324 us
  starting transfers between devices: 21.2 us -> 26.8 us
    psum x1 -> x2, waiting for transfers between devices: 217 us -> 317 us  [shards(): summed = lax.psum(summed, over)]
    ppermute x4, starting transfers between devices: 15 us -> 21.3 us  [with_halo(): after = lax.ppermute(initial, axis, down)]
  transfers between devices with their start and end apart: 9 -> 10, of which waited for: 3 -> 4; matrix products, arithmetic and copies ran while one was open for 12% -> 9% of each run, Pallas kernels for 0% -> 0%
where the time goes in v1:
time: 452 us; the launch traced here: 450 us
  waiting for transfers between devices  324 us (72%)
  other arithmetic  32 us (7%)
  matrix products  28.2 us (6%)
  starting transfers between devices  26.8 us (6%)
  local copies, waits for them, and re-layouts  24.8 us (5%)
  between operations  14.5 us (3%)
    psum x2, waiting for transfers between devices, shards(): summed = lax.psum(summed, over)  317 us
    ppermute x4, starting transfers between devices, with_halo(): after = lax.ppermute(initial, axis, down)  21.3 us
    scatter-add x1, other arithmetic, shards(): jax.ops.segment_sum(grad_inputs[:, feature_width:], edge_dst, num_segment...  10.9 us
    unnamed x46, local copies, waits for them, and re-layouts  10.8 us
    scatter-add x1, other arithmetic, shards(): jax.ops.segment_sum(grad_inputs[:, :feature_width], edge_src, num_segment...  10.6 us
  transfers between devices with their start and end apart: 10, of which 4 were waited for; matrix products, arithmetic and copies ran while one was open for 9% of the time, Pallas kernels for 0%

profile of v1, /device:TPU:2, one launch (start us, length us, event | category | flops | bytes accessed | tf_op | source)
XLA Modules:
  0.0 450.3 jit_solution(6408935485611180460)
XLA Ops:
  8.7 1.8 gather_fusion
  11.2 6.9 %collective-permute-start.1 = (bf16[32,512]{1,0:T(8,128)(2,1)}, bf16[32,512]{1,0:T(8,128)(2,1)S(1)}, u32[]{:S(2)}, u32[]{:S(2)}) collective-permute-start(bf16[32,512]{1,0:T(8,128)(2,1)} %get-tuple-element.21), channel_id=1, source_target_pairs={{1,0},{2,1},{3,2},{4,3},{5,4},{6,5},{7,6},{8,7},{9,8},{10,9},{11,1... | collective-permute-start | bytes 98312 | tf_op jit(solution)/shard_map/ppermute | solution.py:18
  18.1 3.5 collective-permute-start.2
  21.6 4.5 collective-permute-start.3
  27.0 2.7 constant_dynamic-update-slice_fusion.7
  29.7 4.8 %gather_fusion.2 = bf16[1536,512]{1,0:T(8,128)(2,1)S(1)} fusion(bf16[512,512]{1,0:T(8,128)(2,1)S(1)} %bitcast.21, s32[2048]{0:T(1024)S(1)} %pad_clamp_fusion), kind=kCustom, calls=%fused_computation.2 | custom fusion | bytes 3151872 | tf_op jit(solution)/shard_map/gather | solution.py:86
  34.7 5.4 %gather_fusion.1 = bf16[1536,512]{1,0:T(8,128)(2,1)} fusion(bf16[256,512]{1,0:T(8,128)(2,1)S(1)} %constant_dynamic-update-slice_fusion, s32[2048]{0:T(1024)S(1)} %pad_clamp_fusion.1), kind=kCustom, calls=%fused_computation.1 | custom fusion | bytes 3151872 | tf_op jit(solution)/shard_map/gather | solution.py:86
  40.1 2.8 constant_dynamic-update-slice_fusion.6
  44.2 4.5 fusion.69
  56.5 3.6 convolution_convert_fusion
  60.1 3.5 multiply_reduce_fusion
  65.7 2.6 fusion.1
  69.5 4.3 fusion.70
  73.8 271.0 %all-reduce.3.cloned.1.call-done = f32[1536,512]{1,0:T(8,128)} async-done(((f32[1536,512]{1,0:T(8,128)}), f32[1536,512]{1,0:T(8,128)}) %all-reduce.3.cloned.1.call-update) | async-done | bytes 3145744 | tf_op jit(solution)/shard_map/psum | solution.py:139
  344.9 6.2 %fusion.36 = f32[1536,1024]{1,0:T(8,128)} fusion(bf16[1536,512]{1,0:T(8,128)(2,1)} %copy-done.14, bf16[1536,512]{1,0:T(8,128)(2,1)} %param.19), kind=kOutput, calls=%fused_computation.55 | convolution fusion | flops 1610612736 | bytes 8912896 | tf_op jit(solution)/shard_map/dot_general | solution.py:98
  351.1 10.6 %scatter_custom_fusion.1 = f32[256,512]{1,0:T(8,128)S(1)} fusion(s32[1536]{0:T(1024)} %param.16, f32[1536,1024]{1,0:T(8,128)} %fusion.36, f32[]{:T(128)} %constant.22.clone.1), kind=kCustom, calls=%fused_computation.13 | custom fusion | flops 786432 | bytes 3670528 | tf_op jit(solution)/shard_map/scatter-add | solution.py:104
  361.7 5.2 %collective-permute-start.7 = (bf16[32,512]{1,0:T(8,128)(2,1)S(1)}, bf16[32,512]{1,0:T(8,128)(2,1)S(1)}, u32[]{:S(2)}, u32[]{:S(2)}) collective-permute-start(bf16[32,512]{1,0:T(8,128)(2,1)S(1)} %get-tuple-element.10), channel_id=1, source_target_pairs={{32,0},{64,32},{96,64},{128,96},{160,128},{192,160},{224,192},{33,... | collective-permute-start | bytes 98312 | tf_op jit(solution)/shard_map/ppermute | solution.py:18
  366.9 1.9 collective-permute-start.6
  370.1 10.9 %scatter_custom_fusion = f32[512,512]{1,0:T(8,128)S(1)} fusion(f32[512,512]{1,0:T(8,128)S(1)} %convert_add_fusion, s32[1536]{0:T(1024)S(1)} %copy-done.8, f32[1536,1024]{1,0:T(8,128)} %fusion.36), kind=kCustom, calls=%fused_computation.15 | custom fusion | flops 786432 | bytes 4194304 | tf_op jit(solution)/shard_map/scatter-add | solution.py:107
  381.8 4.8 %collective-permute-start.5 = (bf16[32,512]{1,0:T(8,128)(2,1)S(1)}, bf16[32,512]{1,0:T(8,128)(2,1)S(1)}, u32[]{:S(2)}, u32[]{:S(2)}) collective-permute-start(bf16[32,512]{1,0:T(8,128)(2,1)S(1)} %get-tuple-element.12), channel_id=1, source_target_pairs={{1,0},{2,1},{3,2},{4,3},{5,4},{6,5},{7,6},{8,7},{9,8},{10,9},{11,1... | collective-permute-start | bytes 98312 | tf_op jit(solution)/shard_map/ppermute | solution.py:18
  386.7 1.6 collective-permute-done.5
  388.2 5.5 %collective-permute-done.4 = bf16[32,512]{1,0:T(8,128)(2,1)S(1)} collective-permute-done((bf16[32,512]{1,0:T(8,128)(2,1)S(1)}, bf16[32,512]{1,0:T(8,128)(2,1)S(1)}, u32[]{:S(2)}, u32[]{:S(2)}) %collective-permute-start.4) | collective-permute-done | bytes 32800 | tf_op jit(solution)/shard_map/ppermute | solution.py:17
  393.7 1.6 scatter_custom_fusion.2
  396.0 45.9 %all-reduce.5.cloned.1.call-done = f32[1536,512]{1,0:T(8,128)} async-done(((f32[1536,512]{1,0:T(8,128)}), f32[1536,512]{1,0:T(8,128)}) %all-reduce.5.cloned.1.call-update) | async-done | bytes 3145744 | tf_op jit(solution)/shard_map/psum | solution.py:139
  (93 shorter events, 19.9 us)
Async XLA Ops:
  7.2 45.1 %copy-start = (bf16[1024,512]{1,0:T(8,128)(2,1)S(1)}, bf16[1024,512]{1,0:T(8,128)(2,1)}, u32[]{:S(2)}) copy-start(bf16[1024,512]{1,0:T(8,128)(2,1)} %param.22) | copy-start | bytes 3145732
  7.2 22.5 %copy-start.6 = (s32[1536]{0:T(1024)S(1)}, s32[1536]{0:T(1024)}, u32[]{:S(2)}) copy-start(s32[1536]{0:T(1024)} %param.16) | copy-start | bytes 18436
  7.2 22.5 %copy-start.7 = (s32[1536]{0:T(1024)S(1)}, s32[1536]{0:T(1024)}, u32[]{:S(2)}) copy-start(s32[1536]{0:T(1024)} %param.17) | copy-start | bytes 18436
  7.2 22.5 %copy-start.1 = (bf16[8,64,512]{2,1,0:T(8,128)(2,1)S(1)}, bf16[8,64,512]{2,1,0:T(8,128)(2,1)}, u32[]{:S(2)}) copy-start(bf16[8,64,512]{2,1,0:T(8,128)(2,1)} %param.13) | copy-start | bytes 1572868
  7.2 337.6 %all-reduce.3.cloned.1.call-start = ((), (), s32[]{:S(2)}) async-start(), calls=%async_computation | async-start | bytes 6291456 | tf_op jit(solution)/shard_map/psum | solution.py:139
  11.2 23.3 %collective-permute-start = (bf16[32,512]{1,0:T(8,128)(2,1)}, bf16[32,512]{1,0:T(8,128)(2,1)S(1)}, u32[]{:S(2)}, u32[]{:S(2)}) collective-permute-start(bf16[32,512]{1,0:T(8,128)(2,1)} %get-tuple-element.22), channel_id=1, source_target_pairs={{0,1},{1,2},{2,3},{3,4},{4,5},{5,6},{6,7},{7,8},{8,9},{9,10},{10,1... | collective-permute-start | bytes 98312 | tf_op jit(solution)/shard_map/ppermute | solution.py:17
  11.2 23.3 %collective-permute-start.1 = (bf16[32,512]{1,0:T(8,128)(2,1)}, bf16[32,512]{1,0:T(8,128)(2,1)S(1)}, u32[]{:S(2)}, u32[]{:S(2)}) collective-permute-start(bf16[32,512]{1,0:T(8,128)(2,1)} %get-tuple-element.21), channel_id=1, source_target_pairs={{1,0},{2,1},{3,2},{4,3},{5,4},{6,5},{7,6},{8,7},{9,8},{10,9},{11,1... | collective-permute-start | bytes 98312 | tf_op jit(solution)/shard_map/ppermute | solution.py:18
  18.1 16.5 %collective-permute-start.2 = (bf16[32,512]{1,0:T(8,128)(2,1)}, bf16[32,512]{1,0:T(8,128)(2,1)S(1)}, u32[]{:S(2)}, u32[]{:S(2)}) collective-permute-start(bf16[32,512]{1,0:T(8,128)(2,1)} %get-tuple-element.20), channel_id=1, source_target_pairs={{0,32},{32,64},{64,96},{96,128},{128,160},{160,192},{192,224},{1,3... | collective-permute-start | bytes 98312 | tf_op jit(solution)/shard_map/ppermute | solution.py:17
  21.6 13.1 %collective-permute-start.3 = (bf16[32,512]{1,0:T(8,128)(2,1)}, bf16[32,512]{1,0:T(8,128)(2,1)S(1)}, u32[]{:S(2)}, u32[]{:S(2)}) collective-permute-start(bf16[32,512]{1,0:T(8,128)(2,1)} %get-tuple-element.19), channel_id=1, source_target_pairs={{32,0},{64,32},{96,64},{128,96},{160,128},{192,160},{224,192},{33,... | collective-permute-start | bytes 98312 | tf_op jit(solution)/shard_map/ppermute | solution.py:18
  40.1 4.1 copy-start.10
  44.2 4.5 %copy-start.12 = (bf16[512,512]{1,0:T(8,128)(2,1)S(1)}, bf16[512,512]{1,0:T(8,128)(2,1)}, u32[]{:S(2)}) copy-start(bf16[512,512]{1,0:T(8,128)(2,1)} %param.20) | copy-start | bytes 1572868
  48.7 1.6 copy-start.16
  50.4 1.9 copy-start.2
  53.3 1.4 copy-start.4
  53.4 1.4 copy-start.5
  60.1 3.5 copy-start.3
  63.6 2.1 copy-start.17
  63.7 5.8 %slice-start = ((s8[4718592]{0:T(1024)(128)(4,1)}), s8[4194304]{0:T(1024)(128)(4,1)S(1)}, s32[]{:S(2)}) async-start(s8[4718592]{0:T(1024)(128)(4,1)} %bitcast.25), calls=%async_computation.2 | async-start | bytes 8388608
  65.7 3.8 slice-start.1
  73.8 368.2 %all-reduce.5.cloned.1.call-start = ((), (), s32[]{:S(2)}) async-start(), calls=%async_computation.1 | async-start | bytes 6291456 | tf_op jit(solution)/shard_map/psum | solution.py:139
  361.7 24.9 %collective-permute-start.7 = (bf16[32,512]{1,0:T(8,128)(2,1)S(1)}, bf16[32,512]{1,0:T(8,128)(2,1)S(1)}, u32[]{:S(2)}, u32[]{:S(2)}) collective-permute-start(bf16[32,512]{1,0:T(8,128)(2,1)S(1)} %get-tuple-element.10), channel_id=1, source_target_pairs={{32,0},{64,32},{96,64},{128,96},{160,128},{192,160},{224,192},{33,... | collective-permute-start | bytes 98312 | tf_op jit(solution)/shard_map/ppermute | solution.py:18
  366.9 19.7 %collective-permute-start.6 = (bf16[32,512]{1,0:T(8,128)(2,1)S(1)}, bf16[32,512]{1,0:T(8,128)(2,1)S(1)}, u32[]{:S(2)}, u32[]{:S(2)}) collective-permute-start(bf16[32,512]{1,0:T(8,128)(2,1)S(1)} %get-tuple-element.11), channel_id=1, source_target_pairs={{0,32},{32,64},{64,96},{96,128},{128,160},{160,192},{192,224},{1,3... | collective-permute-start | bytes 98312 | tf_op jit(solution)/shard_map/ppermute | solution.py:17
  381.8 6.4 %collective-permute-start.5 = (bf16[32,512]{1,0:T(8,128)(2,1)S(1)}, bf16[32,512]{1,0:T(8,128)(2,1)S(1)}, u32[]{:S(2)}, u32[]{:S(2)}) collective-permute-start(bf16[32,512]{1,0:T(8,128)(2,1)S(1)} %get-tuple-element.12), channel_id=1, source_target_pairs={{1,0},{2,1},{3,2},{4,3},{5,4},{6,5},{7,6},{8,7},{9,8},{10,9},{11,1... | collective-permute-start | bytes 98312 | tf_op jit(solution)/shard_map/ppermute | solution.py:18
  386.6 7.1 %collective-permute-start.4 = (bf16[32,512]{1,0:T(8,128)(2,1)S(1)}, bf16[32,512]{1,0:T(8,128)(2,1)S(1)}, u32[]{:S(2)}, u32[]{:S(2)}) collective-permute-start(bf16[32,512]{1,0:T(8,128)(2,1)S(1)} %get-tuple-element.9), channel_id=1, source_target_pairs={{0,1},{1,2},{2,3},{3,4},{4,5},{5,6},{6,7},{7,8},{8,9},{9,10},{10,1... | collective-permute-start | bytes 98312 | tf_op jit(solution)/shard_map/ppermute | solution.py:17
  (6 other events, 5.7 us)
Sparse Core Ops, SparseCore 0:
  73.9 270.8 all-reduce.2
  347.7 94.1 all-reduce.4
